TPU v7x, 32 devices: a whole 2x2x4 slice. The times are simulated.
32 devices in a mesh: expert: 16 (over z, y, x), dp: 2 (over core).
Axes of the slice: x: 2, y: 2, z: 4, core: 2. Of those that a mesh axis runs over, the one named last changes fastest.
Arguments:
- tokens: bfloat16 [512, 7168], P('expert', 'dp'), may hold values from -6 to 6
- cotangent: bfloat16 [512, 7168], P('expert', 'dp'), may hold values from -6 to 6
- expert_ids: int32 [512, 8], P('expert'), may hold values from 0 to 15, all different within a row; in each aligned block of 32 rows (0 to 31, 32 to 63, ...) at most 32 rows name the same one
- route_weight: float32 [512, 8], P('expert'), may hold values from 0.1 to 1
- gate_weight: bfloat16 [16, 7168, 1024], P('expert', 'dp'), may hold values from -0.0625 to 0.0625
- up_weight: bfloat16 [16, 7168, 1024], P('expert', 'dp'), may hold values from -0.0625 to 0.0625
- down_weight: bfloat16 [16, 7168, 1024], P('expert', 'dp'), may hold values from -0.1875 to 0.1875
Outputs:
- mixed: bfloat16 [512, 7168], P('expert', 'dp')
- grad_tokens: bfloat16 [512, 7168], P('expert', 'dp')
Inputs may be any that keep to these rules, and one draw needn't show every extreme that they name: `expert_ids`: each row names 8 different experts. In the rows of one device (aligned blocks of 32 rows) no expert is named more than 32 times, and in every draw some block names some expert exactly 32 times.
All inputs are finite; a program needn't handle non-finite values.
Results may differ from a plain program's by a relative error of at most 0.028.
Values may be sent and summed in bfloat16 or wider, within the bound.
No kernel may reach another device: no remote copies, remote signals or barrier semaphores. Data moves between devices by JAX's collectives and lax.ppermute only.
A program may use at most 64 MiB of HBM per device.

v0:
```python
import jax
import jax.numpy as jnp
from jax import lax
from jax.sharding import PartitionSpec as P


def local(tokens, cotangent, expert_ids, route_weight, gate_weight, up_weight, down_weight):
    f32, bf16 = (jnp.float32, jnp.bfloat16)
    me = lax.axis_index("expert")
    gate_w = gate_weight[0]
    up_w = up_weight[0]
    down_w = down_weight[0]
    all_tokens = lax.all_gather(tokens, "expert", axis=0, tiled=True)
    all_cot = lax.all_gather(cotangent, "expert", axis=0, tiled=True)
    all_ids = lax.all_gather(expert_ids, "expert", axis=0, tiled=True)
    all_weight = lax.all_gather(route_weight, "expert", axis=0, tiled=True)
    chosen = all_ids == me
    weight = jnp.sum(jnp.where(chosen, all_weight, 0.0), axis=1, keepdims=True)
    named = jnp.any(chosen, axis=1, keepdims=True)
    gate_part = jnp.dot(all_tokens, gate_w, preferred_element_type=f32).astype(bf16)
    up_part = jnp.dot(all_tokens, up_w, preferred_element_type=f32).astype(bf16)
    hidden_part = (weight * jnp.dot(all_cot, down_w, preferred_element_type=f32)).astype(bf16)
    gate = lax.psum(gate_part, "dp").astype(f32)
    up = lax.psum(up_part, "dp").astype(f32)
    hidden_grad = lax.psum(hidden_part, "dp").astype(f32)
    sig = jax.nn.sigmoid(gate)
    hidden = (gate * sig * up).astype(bf16)
    up_grad = (hidden_grad * gate * sig).astype(bf16)
    gate_grad = (hidden_grad * up * sig * (1.0 + gate * (1.0 - sig))).astype(bf16)
    contract = (((1,), (1,)), ((), ()))
    out = (weight * lax.dot_general(hidden, down_w, contract, preferred_element_type=f32)).astype(
        bf16
    )
    grad = lax.dot_general(
        gate_grad, gate_w, contract, preferred_element_type=f32
    ) + lax.dot_general(up_grad, up_w, contract, preferred_element_type=f32)
    grad = jnp.where(named, grad, 0.0).astype(bf16)
    mixed = lax.psum_scatter(out, "expert", scatter_dimension=0, tiled=True)
    grad_tokens = lax.psum_scatter(grad, "expert", scatter_dimension=0, tiled=True)
    return (mixed, grad_tokens)


def solution(mesh):
    return jax.shard_map(
        local,
        mesh=mesh,
        in_specs=(
            P("expert", "dp"),
            P("expert", "dp"),
            P("expert", None),
            P("expert", None),
            P("expert", "dp", None),
            P("expert", "dp", None),
            P("expert", "dp", None),
        ),
        out_specs=(P("expert", "dp"), P("expert", "dp")),
        check_vma=False,
    )
```

profile of v0, /device:TPU:0, one launch (start us, length us, event | category | flops | bytes accessed | tf_op | source)
XLA Modules:
  0.0 392.5 jit_solution(4316116910010661094)
XLA Ops:
  7.2 0.0 all-gather.5.cloned.1.call-start
  7.2 0.7 all-gather.5.cloned.1.call-update
  7.9 0.0 all-gather.7.cloned.1.call-start
  7.9 0.7 all-gather.7.cloned.1.call-update
  8.6 0.0 all-reduce.3.cloned.1.call-start
  8.7 43.4 %all-gather = s32[16,32,8]{1,2,0:T(8,128)S(1)} all-gather(s32[1,32,8]{1,2,0:T(8,128)} %bitcast.30), channel_id=1, replica_groups=mesh['expert'=16,'dp'=2] {'expert'}, dimensions={0}, use_global_device_ids=true | all-gather | bytes 17408 | tf_op jit(solution)/shard_map/all_gather | solution.py:15
  52.1 37.4 %all-gather.1 = f32[16,32,8]{1,2,0:T(8,128)S(1)} all-gather(f32[1,32,8]{1,2,0:T(8,128)} %bitcast.31), channel_id=1, replica_groups=mesh['expert'=16,'dp'=2] {'expert'}, dimensions={0}, use_global_device_ids=true | all-gather | bytes 17408 | tf_op jit(solution)/shard_map/all_gather | solution.py:16
  89.6 0.1 reshape.15
  89.6 0.0 all-gather.5.cloned.1.call-done
  89.6 0.0 copy-start
  89.6 9.3 %fusion.28 = bf16[512,1024]{1,0:T(8,128)(2,1)} fusion(bf16[512,3584]{1,0:T(8,128)(2,1)} %all-gather.5.cloned.1.call-done, bf16[1,3584,1024]{2,1,0:T(8,128)(2,1)} %param.11), kind=kOutput, calls=%fused_computation.31 | convolution fusion | flops 3758620672 | bytes 12058624 | tf_op jit(solution)/shard_map/dot_general | solution.py:20
  98.9 0.0 copy-done
  98.9 7.4 %fusion.31 = bf16[512,1024]{1,0:T(8,128)(2,1)} fusion(bf16[512,3584]{1,0:T(8,128)(2,1)S(1)} %copy-done, bf16[1,3584,1024]{2,1,0:T(8,128)(2,1)} %param.12), kind=kOutput, calls=%fused_computation.32 | convolution fusion | flops 3758620672 | bytes 12058624 | tf_op jit(solution)/shard_map/dot_general | solution.py:21
  106.3 52.5 %all-gather.7.cloned.1.call-done = bf16[512,3584]{1,0:T(8,128)(2,1)} async-done(((bf16[32,3584]{1,0:T(8,128)(2,1)}), bf16[512,3584]{1,0:T(8,128)(2,1)}) %all-gather.7.cloned.1.call-update) | async-done | bytes 3670032 | tf_op jit(solution)/shard_map/all_gather | solution.py:14
  158.8 9.2 %multiply_convert_fusion.1 = bf16[512,1024]{1,0:T(8,128)(2,1)} fusion(bf16[512,3584]{1,0:T(8,128)(2,1)} %all-gather.7.cloned.1.call-done, bf16[1,3584,1024]{2,1,0:T(8,128)(2,1)} %param.13, f32[512]{0:T(512)S(1)} %reshape.15), kind=kOutput, calls=%fused_computation.30 | convolution fusion | flops 3759144960 | bytes 12060672 | tf_op jit(solution)/shard_map/dot_general | solution.py:22
  168.0 0.0 all-reduce.3.cloned.1.call-update
  168.0 0.2 reduce-scatter.5.cloned.1.call-start
  168.2 0.1 reshape.12
  168.3 21.9 %all-reduce.3.cloned.1.call-done = (bf16[512,1024]{1,0:T(8,128)(2,1)}, bf16[512,1024]{1,0:T(8,128)(2,1)}, bf16[512,1024]{1,0:T(8,128)(2,1)}) async-done(((bf16[512,1024]{1,0:T(8,128)(2,1)}, bf16[512,1024]{1,0:T(8,128)(2,1)}, bf16[512,1024]{1,0:T(8,128)(2,1)}), (bf16[512,1024]{1,0:T(8,128)(2,1)}, bf16[512,1024]{1,0:T(8,128)(2,1)}, bf16[512,1024]{1,0:T(8,128)(2,1)})) %all-reduce.3.cloned.1.call-update) | async-done | bytes 3145744 | tf_op jit(solution)/shard_map/psum | solution.py:24
  190.2 0.0 copy-start.1
  190.2 0.0 copy-start.2
  190.2 0.0 copy-start.3
  190.2 10.9 %fusion.4 = f32[512,3584]{1,0:T(8,128)} fusion(bf16[1,3584,1024]{2,1,0:T(8,128)(2,1)} %param.12, bf16[512,1024]{1,0:T(8,128)(2,1)} %get-tuple-element.3, bf16[512,1024]{1,0:T(8,128)(2,1)} %get-tuple-element.4), kind=kOutput, calls=%fused_computation.4 | convolution fusion | flops 3762290688 | bytes 16777216 | tf_op jit(solution)/shard_map/dot_general | solution.py:36
  201.1 0.0 copy-done.1
  201.1 0.0 copy-done.2
  201.2 0.0 copy-done.3
  201.2 10.3 %select_convert_fusion = bf16[512,3584]{1,0:T(8,128)(2,1)} fusion(f32[512,3584]{1,0:T(8,128)} %fusion.4, bf16[1,3584,1024]{2,1,0:T(8,128)(2,1)} %param.11, pred[512]{0:T(512)(128)(4,1)S(1)} %reshape.12, bf16[512,1024]{1,0:T(8,128)(2,1)S(1)} %copy-done.1, bf16[512,1024]{1,0:T(8,128)(2,1)S(1)} %copy-done.3, bf16[512,1024]{1,0:T(8,128)(2,1)S(1)} %copy-done.2), kind=kOutput, calls=%fused_computation.12 | convolution fusion | flops 3770417152 | bytes 21496320 | tf_op jit(solution)/shard_map/dot_general | solution.py:34
  211.5 0.0 reduce-scatter.5.cloned.1.call-update
  211.5 0.0 reduce-scatter.3.cloned.1.call-start
  211.5 8.8 %multiply_convert_fusion = bf16[512,3584]{1,0:T(8,128)(2,1)} fusion(bf16[1,3584,1024]{2,1,0:T(8,128)(2,1)} %param.13, f32[512]{0:T(512)S(1)} %reshape.15, bf16[512,1024]{1,0:T(8,128)(2,1)S(1)} %copy-done.1, bf16[512,1024]{1,0:T(8,128)(2,1)S(1)} %copy-done.2), kind=kOutput, calls=%fused_computation.13 | convolution fusion | flops 3765960704 | bytes 13109248 | tf_op jit(solution)/shard_map/dot_general | solution.py:31
  220.3 0.0 reduce-scatter.3.cloned.1.call-update
  220.3 78.2 %reduce-scatter.5.cloned.1.call-done = bf16[32,3584]{1,0:T(8,128)(2,1)} async-done(((bf16[512,3584]{1,0:T(8,128)(2,1)}), bf16[32,3584]{1,0:T(8,128)(2,1)}) %reduce-scatter.5.cloned.1.call-update) | async-done | bytes 229392 | tf_op jit(solution)/shard_map/reduce_scatter | solution.py:39
  298.5 87.5 %reduce-scatter.3.cloned.1.call-done = bf16[32,3584]{1,0:T(8,128)(2,1)} async-done(((bf16[512,3584]{1,0:T(8,128)(2,1)}), bf16[32,3584]{1,0:T(8,128)(2,1)}) %reduce-scatter.3.cloned.1.call-update) | async-done | bytes 229392 | tf_op jit(solution)/shard_map/reduce_scatter | solution.py:38
  (2 shorter events, 0.1 us)
Async XLA Ops:
  7.2 82.5 %all-gather.5.cloned.1.call-start = ((), (), s32[]{:S(2)}) async-start(), calls=%async_computation.2 | async-start | bytes 3899392 | tf_op jit(solution)/shard_map/all_gather | solution.py:13
  7.9 150.9 %all-gather.7.cloned.1.call-start = ((), (), s32[]{:S(2)}) async-start(), calls=%async_computation.4 | async-start | bytes 3899392 | tf_op jit(solution)/shard_map/all_gather | solution.py:14
  8.6 181.6 %all-reduce.3.cloned.1.call-start = ((), (), s32[]{:S(2)}) async-start(), calls=%async_computation.6 | async-start | bytes 6291456 | tf_op jit(solution)/shard_map/psum | solution.py:24
  89.6 9.3 %copy-start = (bf16[512,3584]{1,0:T(8,128)(2,1)S(1)}, bf16[512,3584]{1,0:T(8,128)(2,1)}, u32[]{:S(2)}) copy-start(bf16[512,3584]{1,0:T(8,128)(2,1)} %all-gather.5.cloned.1.call-done) | copy-start | bytes 11010052
  168.0 130.5 %reduce-scatter.5.cloned.1.call-start = ((), (), s32[]{:S(2)}) async-start(), calls=%async_computation.5 | async-start | bytes 3899392 | tf_op jit(solution)/shard_map/reduce_scatter | solution.py:39
  190.2 10.9 %copy-start.1 = (bf16[512,1024]{1,0:T(8,128)(2,1)S(1)}, bf16[512,1024]{1,0:T(8,128)(2,1)}, u32[]{:S(2)}) copy-start(bf16[512,1024]{1,0:T(8,128)(2,1)} %get-tuple-element.2) | copy-start | bytes 3145732
  190.2 10.9 %copy-start.2 = (bf16[512,1024]{1,0:T(8,128)(2,1)S(1)}, bf16[512,1024]{1,0:T(8,128)(2,1)}, u32[]{:S(2)}) copy-start(bf16[512,1024]{1,0:T(8,128)(2,1)} %get-tuple-element.3) | copy-start | bytes 3145732
  190.2 10.9 %copy-start.3 = (bf16[512,1024]{1,0:T(8,128)(2,1)S(1)}, bf16[512,1024]{1,0:T(8,128)(2,1)}, u32[]{:S(2)}) copy-start(bf16[512,1024]{1,0:T(8,128)(2,1)} %get-tuple-element.4) | copy-start | bytes 3145732
  211.5 174.5 %reduce-scatter.3.cloned.1.call-start = ((), (), s32[]{:S(2)}) async-start(), calls=%async_computation.3 | async-start | bytes 3899392 | tf_op jit(solution)/shard_map/reduce_scatter | solution.py:38
Sparse Core Ops, SparseCore 0:
  10.7 74.9 all-gather.4
  88.5 70.2 all-gather.6
  168.1 22.0 all-reduce.2
  211.6 86.8 reduce-scatter.4
  301.3 84.6 reduce-scatter.2
where the time goes:
time: 393 us
  waiting for transfers between devices  241 us (61%)
  blocking collectives  80.8 us (21%)
  matrix products  55.9 us (14%)
  between operations  13.8 us (4%)
    reduce_scatter x1, waiting for transfers between devices, local(): mixed = lax.psum_scatter(out, 'expert', scatter_dimension=0, tiled=True)  87.5 us
    reduce_scatter x1, waiting for transfers between devices, local(): lax.psum_scatter(grad, 'expert', scatter_dimension=0, tiled=True)  78.2 us
    all_gather x1, waiting for transfers between devices, local(): all_cot = lax.all_gather(cotangent, 'expert', axis=0, tiled=True)  52.5 us
    all_gather x1, blocking collectives, local(): all_ids = lax.all_gather(expert_ids, 'expert', axis=0, tiled=True)  43.4 us
    all_gather x1, blocking collectives, local(): all_weight = lax.all_gather(route_weight, 'expert', axis=0, tiled=True)  37.4 us
    psum x1, waiting for transfers between devices, local(): up = lax.psum(up_part, 'dp').astype(f32)  21.9 us
    dot_general x1, matrix products, local(): lax.dot_general(up_grad, up_w, contract, preferred_element_type=f32)  10.9 us
    dot_general x1, matrix products, local(): lax.dot_general(gate_grad, gate_w, contract, preferred_element_type=f32)  10.3 us
  transfers between devices with their start and end apart: 5, of which 4 were waited for; matrix products, arithmetic and copies ran while one was open for 7% of the time, Pallas kernels for 0%

commit v1 on v0

--- a/solution.py
+++ b/solution.py
@@ -2,6 +2,18 @@
 import jax.numpy as jnp
 from jax import lax
 from jax.sharding import PartitionSpec as P
+
+
+def collect(array, axis, dim):
+    ways, here, turn = (lax.axis_size(axis), lax.axis_index(axis), array.shape[dim])
+    shape = [n * ways if d == dim else n for d, n in enumerate(array.shape)]
+    full = lax.dynamic_update_slice_in_dim(
+        jnp.zeros(shape, array.dtype), array, here * turn, axis=dim
+    )
+    for far in range(1, ways):
+        array = lax.ppermute(array, axis, [(d, (d + 1) % ways) for d in range(ways)])
+        full = lax.dynamic_update_slice_in_dim(full, array, (here - far) % ways * turn, axis=dim)
+    return full
 
 
 def local(tokens, cotangent, expert_ids, route_weight, gate_weight, up_weight, down_weight):
@@ -12,7 +24,7 @@
     down_w = down_weight[0]
     all_tokens = lax.all_gather(tokens, "expert", axis=0, tiled=True)
     all_cot = lax.all_gather(cotangent, "expert", axis=0, tiled=True)
-    all_ids = lax.all_gather(expert_ids, "expert", axis=0, tiled=True)
+    all_ids = collect(expert_ids, "expert", 0)
     all_weight = lax.all_gather(route_weight, "expert", axis=0, tiled=True)
     chosen = all_ids == me
     weight = jnp.sum(jnp.where(chosen, all_weight, 0.0), axis=1, keepdims=True)

time: 393 us -> 394 us (level)
  blocking collectives: 80.8 us -> 40.5 us
  waiting for transfers between devices: 241 us -> 275 us
  local copies, waits for them, and re-layouts: 0.18 us -> 4.85 us
    ppermute x0 -> x15, waiting for transfers between devices: none -> 97.1 us  [collect(): lax.ppermute(array, axis, [(d, (d + 1) % ways) for d in range(ways)])]
    all_gather x1, waiting for transfers between devices: 52.5 us -> 0.01 us  [local(): all_cot = lax.all_gather(cotangent, 'expert', axis=0, tiled=True)]
    all_gather x1 -> x0, blocking collectives: 43.4 us -> none  [local(): all_ids = lax.all_gather(expert_ids, 'expert', axis=0, tiled=True)]
    reduce_scatter x1, waiting for transfers between devices: 87.5 us -> 67 us  [local(): mixed = lax.psum_scatter(out, 'expert', scatter_dimension=0, tiled=True)]
    reduce_scatter x1, waiting for transfers between devices: 78.2 us -> 87.3 us  [local(): lax.psum_scatter(grad, 'expert', scatter_dimension=0, tiled=True)]
    dynamic_update_slice x0 -> x16, local copies, waits for them, and re-layouts: none -> 4.72 us  [the longest x15 3.94 us: collect(): lax.dynamic_update_slice_in_dim(full, array, (here - far) % ways * turn,...]
  transfers between devices with their start and end apart: 5 -> 20, of which waited for: 4 -> 17; matrix products, arithmetic and copies ran while one was open for 7% -> 11% of each run, Pallas kernels for 0% -> 0%
where the time goes in v1:
time: 394 us
  waiting for transfers between devices  275 us (70%)
  matrix products  55.7 us (14%)
  blocking collectives  40.5 us (10%)
  between operations  14 us (4%)
  local copies, waits for them, and re-layouts  4.85 us (1%)
    ppermute x15, waiting for transfers between devices, collect(): lax.ppermute(array, axis, [(d, (d + 1) % ways) for d in range(ways)])  97.1 us
    reduce_scatter x1, waiting for transfers between devices, local(): lax.psum_scatter(grad, 'expert', scatter_dimension=0, tiled=True)  87.3 us
    reduce_scatter x1, waiting for transfers between devices, local(): mixed = lax.psum_scatter(out, 'expert', scatter_dimension=0, tiled=True)  67 us
    all_gather x1, blocking collectives, local(): all_weight = lax.all_gather(route_weight, 'expert', axis=0, tiled=True)  40.5 us
    psum x1, waiting for transfers between devices, local(): up = lax.psum(up_part, 'dp').astype(f32)  22.3 us
    dot_general x1, matrix products, local(): lax.dot_general(gate_grad, gate_w, contract, preferred_element_type=f32)  11.6 us
    dot_general x1, matrix products, local(): lax.dot_general(hidden, down_w, contract, preferred_element_type=f32)  9.84 us
    dot_general x1, matrix products, local(): up_part = jnp.dot(all_tokens, up_w, preferred_element_type=f32).astype(bf16)  9.35 us
  transfers between devices with their start and end apart: 20, of which 17 were waited for; matrix products, arithmetic and copies ran while one was open for 11% of the time, Pallas kernels for 0%

profile of v1, /device:TPU:0, one launch (start us, length us, event | category | flops | bytes accessed | tf_op | source)
XLA Modules:
  0.0 393.6 jit_solution(7852412366992350281)
XLA Ops:
  7.2 0.0 all-gather.4.cloned.1.call-start
  7.2 0.7 all-gather.4.cloned.1.call-update
  7.9 0.0 all-gather.6.cloned.1.call-start
  7.9 0.7 all-gather.6.cloned.1.call-update
  8.6 0.0 all-reduce.3.cloned.1.call-start
  8.7 3.0 collective-permute-start
  11.7 40.5 %all-gather = f32[16,32,8]{1,2,0:T(8,128)S(1)} all-gather(f32[1,32,8]{1,2,0:T(8,128)} %bitcast.31), channel_id=1, replica_groups=mesh['expert'=16,'dp'=2] {'expert'}, dimensions={0}, use_global_device_ids=true | all-gather | bytes 17408 | tf_op jit(solution)/shard_map/all_gather | solution.py:28
  52.2 0.0 collective-permute-done
  52.2 0.0 collective-permute-start.1
  52.2 7.2 %collective-permute-done.1 = s32[32,8]{0,1:T(8,128)S(1)} collective-permute-done((s32[32,8]{0,1:T(8,128)S(1)}, s32[32,8]{0,1:T(8,128)S(1)}, u32[]{:S(2)}, u32[]{:S(2)}) %collective-permute-start.1) | collective-permute-done | bytes 1056 | tf_op jit(solution)/shard_map/ppermute | solution.py:14
  59.4 0.0 collective-permute-start.2
  59.4 7.3 %collective-permute-done.2 = s32[32,8]{0,1:T(8,128)S(1)} collective-permute-done((s32[32,8]{0,1:T(8,128)S(1)}, s32[32,8]{0,1:T(8,128)S(1)}, u32[]{:S(2)}, u32[]{:S(2)}) %collective-permute-start.2) | collective-permute-done | bytes 1056 | tf_op jit(solution)/shard_map/ppermute | solution.py:14
  66.7 0.0 collective-permute-start.3
  66.7 7.4 %collective-permute-done.3 = s32[32,8]{0,1:T(8,128)S(1)} collective-permute-done((s32[32,8]{0,1:T(8,128)S(1)}, s32[32,8]{0,1:T(8,128)S(1)}, u32[]{:S(2)}, u32[]{:S(2)}) %collective-permute-start.3) | collective-permute-done | bytes 1056 | tf_op jit(solution)/shard_map/ppermute | solution.py:14
  74.2 0.0 collective-permute-start.4
  74.2 7.2 %collective-permute-done.4 = s32[32,8]{0,1:T(8,128)S(1)} collective-permute-done((s32[32,8]{0,1:T(8,128)S(1)}, s32[32,8]{0,1:T(8,128)S(1)}, u32[]{:S(2)}, u32[]{:S(2)}) %collective-permute-start.4) | collective-permute-done | bytes 1056 | tf_op jit(solution)/shard_map/ppermute | solution.py:14
  81.4 0.0 collective-permute-start.5
  81.4 7.2 %collective-permute-done.5 = s32[32,8]{0,1:T(8,128)S(1)} collective-permute-done((s32[32,8]{0,1:T(8,128)S(1)}, s32[32,8]{0,1:T(8,128)S(1)}, u32[]{:S(2)}, u32[]{:S(2)}) %collective-permute-start.5) | collective-permute-done | bytes 1056 | tf_op jit(solution)/shard_map/ppermute | solution.py:14
  88.6 7.2 %collective-permute-done.6 = s32[32,8]{0,1:T(8,128)S(1)} collective-permute-done((s32[32,8]{0,1:T(8,128)S(1)}, s32[32,8]{0,1:T(8,128)S(1)}, u32[]{:S(2)}, u32[]{:S(2)}) %collective-permute-start.6) | collective-permute-done | bytes 1056 | tf_op jit(solution)/shard_map/ppermute | solution.py:14
  95.8 7.2 %collective-permute-done.7 = s32[32,8]{0,1:T(8,128)S(1)} collective-permute-done((s32[32,8]{0,1:T(8,128)S(1)}, s32[32,8]{0,1:T(8,128)S(1)}, u32[]{:S(2)}, u32[]{:S(2)}) %collective-permute-start.7) | collective-permute-done | bytes 1056 | tf_op jit(solution)/shard_map/ppermute | solution.py:14
  103.0 0.0 collective-permute-start.8
  103.0 7.2 %collective-permute-done.8 = s32[32,8]{0,1:T(8,128)S(1)} collective-permute-done((s32[32,8]{0,1:T(8,128)S(1)}, s32[32,8]{0,1:T(8,128)S(1)}, u32[]{:S(2)}, u32[]{:S(2)}) %collective-permute-start.8) | collective-permute-done | bytes 1056 | tf_op jit(solution)/shard_map/ppermute | solution.py:14
  110.2 0.0 collective-permute-start.9
  110.2 7.3 %collective-permute-done.9 = s32[32,8]{0,1:T(8,128)S(1)} collective-permute-done((s32[32,8]{0,1:T(8,128)S(1)}, s32[32,8]{0,1:T(8,128)S(1)}, u32[]{:S(2)}, u32[]{:S(2)}) %collective-permute-start.9) | collective-permute-done | bytes 1056 | tf_op jit(solution)/shard_map/ppermute | solution.py:14
  117.5 0.0 collective-permute-start.10
  117.5 7.2 %collective-permute-done.10 = s32[32,8]{0,1:T(8,128)S(1)} collective-permute-done((s32[32,8]{0,1:T(8,128)S(1)}, s32[32,8]{0,1:T(8,128)S(1)}, u32[]{:S(2)}, u32[]{:S(2)}) %collective-permute-start.10) | collective-permute-done | bytes 1056 | tf_op jit(solution)/shard_map/ppermute | solution.py:14
  124.7 0.0 collective-permute-start.11
  124.7 7.2 %collective-permute-done.11 = s32[32,8]{0,1:T(8,128)S(1)} collective-permute-done((s32[32,8]{0,1:T(8,128)S(1)}, s32[32,8]{0,1:T(8,128)S(1)}, u32[]{:S(2)}, u32[]{:S(2)}) %collective-permute-start.11) | collective-permute-done | bytes 1056 | tf_op jit(solution)/shard_map/ppermute | solution.py:14
  131.9 7.4 %collective-permute-done.12 = s32[32,8]{0,1:T(8,128)S(1)} collective-permute-done((s32[32,8]{0,1:T(8,128)S(1)}, s32[32,8]{0,1:T(8,128)S(1)}, u32[]{:S(2)}, u32[]{:S(2)}) %collective-permute-start.12) | collective-permute-done | bytes 1056 | tf_op jit(solution)/shard_map/ppermute | solution.py:14
  139.4 0.1 reshape.7
  139.5 7.2 %collective-permute-done.13 = s32[32,8]{0,1:T(8,128)S(1)} collective-permute-done((s32[32,8]{0,1:T(8,128)S(1)}, s32[32,8]{0,1:T(8,128)S(1)}, u32[]{:S(2)}, u32[]{:S(2)}) %collective-permute-start.13) | collective-permute-done | bytes 1056 | tf_op jit(solution)/shard_map/ppermute | solution.py:14
  146.8 0.8 dynamic_update_slice.48
  147.6 0.3 dynamic_update_slice.49
  147.8 0.2 dynamic_update_slice.50
  148.1 0.2 dynamic_update_slice.51
  148.3 0.2 dynamic_update_slice.52
  148.5 0.3 dynamic_update_slice.53
  148.8 0.3 dynamic_update_slice.54
  149.1 0.3 dynamic_update_slice.55
  149.4 0.2 dynamic_update_slice.56
  149.6 0.3 dynamic_update_slice.57
  149.9 0.3 dynamic_update_slice.58
  150.2 0.3 dynamic_update_slice.59
  150.5 0.2 dynamic_update_slice.60
  150.8 0.3 dynamic_update_slice.61
  151.1 0.3 dynamic_update_slice.62
  151.4 2.7 collective-permute-done.14
  154.1 0.2 dynamic_update_slice.63
  154.3 0.0 all-gather.4.cloned.1.call-done
  154.3 9.4 %fusion.25 = bf16[512,1024]{1,0:T(8,128)(2,1)} fusion(bf16[512,3584]{1,0:T(8,128)(2,1)} %all-gather.4.cloned.1.call-done, bf16[1,3584,1024]{2,1,0:T(8,128)(2,1)} %param.12), kind=kOutput, calls=%fused_computation.32 | convolution fusion | flops 3758620672 | bytes 12058624 | tf_op jit(solution)/shard_map/dot_general | solution.py:33
  163.7 7.5 %fusion.22 = bf16[512,1024]{1,0:T(8,128)(2,1)} fusion(bf16[512,3584]{1,0:T(8,128)(2,1)S(1)} %copy-done, bf16[1,3584,1024]{2,1,0:T(8,128)(2,1)} %param.11), kind=kOutput, calls=%fused_computation.31 | convolution fusion | flops 3758620672 | bytes 12058624 | tf_op jit(solution)/shard_map/dot_general | solution.py:32
  171.2 9.1 %multiply_convert_fusion.1 = bf16[512,1024]{1,0:T(8,128)(2,1)} fusion(f32[512]{0:T(512)S(1)} %select_reduce_fusion, bf16[512,3584]{1,0:T(8,128)(2,1)} %all-gather.6.cloned.1.call-done, bf16[1,3584,1024]{2,1,0:T(8,128)(2,1)} %param.13), kind=kOutput, calls=%fused_computation.30 | convolution fusion | flops 3759144960 | bytes 12060672 | tf_op jit(solution)/shard_map/dot_general | solution.py:34
  180.3 0.0 all-reduce.3.cloned.1.call-update
  180.3 0.2 reduce-scatter.3.cloned.1.call-start
  180.5 22.3 %all-reduce.3.cloned.1.call-done = (bf16[512,1024]{1,0:T(8,128)(2,1)}, bf16[512,1024]{1,0:T(8,128)(2,1)}, bf16[512,1024]{1,0:T(8,128)(2,1)}) async-done(((bf16[512,1024]{1,0:T(8,128)(2,1)}, bf16[512,1024]{1,0:T(8,128)(2,1)}, bf16[512,1024]{1,0:T(8,128)(2,1)}), (bf16[512,1024]{1,0:T(8,128)(2,1)}, bf16[512,1024]{1,0:T(8,128)(2,1)}, bf16[512,1024]{1,0:T(8,128)(2,1)})) %all-reduce.3.cloned.1.call-update) | async-done | bytes 3145744 | tf_op jit(solution)/shard_map/psum | solution.py:36
  202.8 9.8 %multiply_convert_fusion = bf16[512,3584]{1,0:T(8,128)(2,1)} fusion(f32[512]{0:T(512)S(1)} %select_reduce_fusion, bf16[1,3584,1024]{2,1,0:T(8,128)(2,1)} %param.13, bf16[512,1024]{1,0:T(8,128)(2,1)} %get-tuple-element.2, bf16[512,1024]{1,0:T(8,128)(2,1)} %get-tuple-element.3), kind=kOutput, calls=%fused_computation.13 | convolution fusion | flops 3765960704 | bytes 13109248 | tf_op jit(solution)/shard_map/dot_general | solution.py:43
  212.7 0.0 reduce-scatter.3.cloned.1.call-update
  212.7 0.0 reduce-scatter.5.cloned.1.call-start
  212.8 0.0 slice-start.1
  212.8 11.6 %fusion.8 = f32[512,3584]{1,0:T(8,128)} fusion(bf16[1,3584,1024]{2,1,0:T(8,128)(2,1)} %param.11, bf16[512,1024]{1,0:T(8,128)(2,1)} %get-tuple-element.2, bf16[512,1024]{1,0:T(8,128)(2,1)} %get-tuple-element.4, bf16[512,1024]{1,0:T(8,128)(2,1)} %get-tuple-element.3), kind=kOutput, calls=%fused_computation.8 | convolution fusion | flops 3764912128 | bytes 17825792 | tf_op jit(solution)/shard_map/dot_general | solution.py:46
  224.4 8.3 %select_convert_fusion = bf16[512,3584]{1,0:T(8,128)(2,1)} fusion(f32[512,3584]{1,0:T(8,128)} %fusion.8, pred[512]{0:T(512)(128)(4,1)S(1)} %get-tuple-element.5, bf16[1,3584,1024]{2,1,0:T(8,128)(2,1)S(1)} %bitcast.33, bf16[512,1024]{1,0:T(8,128)(2,1)S(1)} %copy-done.1, bf16[512,1024]{1,0:T(8,128)(2,1)S(1)} %copy-done.2), kind=kOutput, calls=%fused_computation.12 | convolution fusion | flops 3767795712 | bytes 20447744 | tf_op jit(solution)/shard_map/dot_general | solution.py:48
  232.7 0.0 reduce-scatter.5.cloned.1.call-update
  232.7 67.0 %reduce-scatter.3.cloned.1.call-done = bf16[32,3584]{1,0:T(8,128)(2,1)} async-done(((bf16[512,3584]{1,0:T(8,128)(2,1)}), bf16[32,3584]{1,0:T(8,128)(2,1)}) %reduce-scatter.3.cloned.1.call-update) | async-done | bytes 229392 | tf_op jit(solution)/shard_map/reduce_scatter | solution.py:50
  299.8 87.3 %reduce-scatter.5.cloned.1.call-done = bf16[32,3584]{1,0:T(8,128)(2,1)} async-done(((bf16[512,3584]{1,0:T(8,128)(2,1)}), bf16[32,3584]{1,0:T(8,128)(2,1)}) %reduce-scatter.5.cloned.1.call-update) | async-done | bytes 229392 | tf_op jit(solution)/shard_map/reduce_scatter | solution.py:51
  (20 shorter events, 0.1 us)
Async XLA Ops:
  7.2 147.2 %all-gather.4.cloned.1.call-start = ((), (), s32[]{:S(2)}) async-start(), calls=%async_computation.2 | async-start | bytes 3899392 | tf_op jit(solution)/shard_map/all_gather | solution.py:25
  7.9 163.3 %all-gather.6.cloned.1.call-start = ((), (), s32[]{:S(2)}) async-start(), calls=%async_computation.4 | async-start | bytes 3899392 | tf_op jit(solution)/shard_map/all_gather | solution.py:26
  8.6 194.2 %all-reduce.3.cloned.1.call-start = ((), (), s32[]{:S(2)}) async-start(), calls=%async_computation.6 | async-start | bytes 6291456 | tf_op jit(solution)/shard_map/psum | solution.py:36
  8.7 43.5 %collective-permute-start = (s32[32,8]{0,1:T(8,128)}, s32[32,8]{0,1:T(8,128)S(1)}, u32[]{:S(2)}, u32[]{:S(2)}) collective-permute-start(s32[32,8]{0,1:T(8,128)} %param.9), channel_id=1, source_target_pairs={{0,2},{2,4},{4,6},{6,8},{8,10},{10,12},{12,14},{14,16},{16,18},{18... | collective-permute-start | bytes 3080 | tf_op jit(solution)/shard_map/ppermute | solution.py:14
  52.2 7.2 %collective-permute-start.1 = (s32[32,8]{0,1:T(8,128)S(1)}, s32[32,8]{0,1:T(8,128)S(1)}, u32[]{:S(2)}, u32[]{:S(2)}) collective-permute-start(s32[32,8]{0,1:T(8,128)S(1)} %collective-permute-done), channel_id=1, source_target_pairs={{0,2},{2,4},{4,6},{6,8},{8,10},{10,12},{12,14},{14,16},{16,18},{18... | collective-permute-start | bytes 3080 | tf_op jit(solution)/shard_map/ppermute | solution.py:14
  59.4 7.3 %collective-permute-start.2 = (s32[32,8]{0,1:T(8,128)S(1)}, s32[32,8]{0,1:T(8,128)S(1)}, u32[]{:S(2)}, u32[]{:S(2)}) collective-permute-start(s32[32,8]{0,1:T(8,128)S(1)} %collective-permute-done.1), channel_id=1, source_target_pairs={{0,2},{2,4},{4,6},{6,8},{8,10},{10,12},{12,14},{14,16},{16,18},{18... | collective-permute-start | bytes 3080 | tf_op jit(solution)/shard_map/ppermute | solution.py:14
  66.7 7.4 %collective-permute-start.3 = (s32[32,8]{0,1:T(8,128)S(1)}, s32[32,8]{0,1:T(8,128)S(1)}, u32[]{:S(2)}, u32[]{:S(2)}) collective-permute-start(s32[32,8]{0,1:T(8,128)S(1)} %collective-permute-done.2), channel_id=1, source_target_pairs={{0,2},{2,4},{4,6},{6,8},{8,10},{10,12},{12,14},{14,16},{16,18},{18... | collective-permute-start | bytes 3080 | tf_op jit(solution)/shard_map/ppermute | solution.py:14
  74.2 7.2 %collective-permute-start.4 = (s32[32,8]{0,1:T(8,128)S(1)}, s32[32,8]{0,1:T(8,128)S(1)}, u32[]{:S(2)}, u32[]{:S(2)}) collective-permute-start(s32[32,8]{0,1:T(8,128)S(1)} %collective-permute-done.3), channel_id=1, source_target_pairs={{0,2},{2,4},{4,6},{6,8},{8,10},{10,12},{12,14},{14,16},{16,18},{18... | collective-permute-start | bytes 3080 | tf_op jit(solution)/shard_map/ppermute | solution.py:14
  81.4 7.2 %collective-permute-start.5 = (s32[32,8]{0,1:T(8,128)S(1)}, s32[32,8]{0,1:T(8,128)S(1)}, u32[]{:S(2)}, u32[]{:S(2)}) collective-permute-start(s32[32,8]{0,1:T(8,128)S(1)} %collective-permute-done.4), channel_id=1, source_target_pairs={{0,2},{2,4},{4,6},{6,8},{8,10},{10,12},{12,14},{14,16},{16,18},{18... | collective-permute-start | bytes 3080 | tf_op jit(solution)/shard_map/ppermute | solution.py:14
  88.6 7.2 %collective-permute-start.6 = (s32[32,8]{0,1:T(8,128)S(1)}, s32[32,8]{0,1:T(8,128)S(1)}, u32[]{:S(2)}, u32[]{:S(2)}) collective-permute-start(s32[32,8]{0,1:T(8,128)S(1)} %collective-permute-done.5), channel_id=1, source_target_pairs={{0,2},{2,4},{4,6},{6,8},{8,10},{10,12},{12,14},{14,16},{16,18},{18... | collective-permute-start | bytes 3080 | tf_op jit(solution)/shard_map/ppermute | solution.py:14
  95.8 7.2 %collective-permute-start.7 = (s32[32,8]{0,1:T(8,128)S(1)}, s32[32,8]{0,1:T(8,128)S(1)}, u32[]{:S(2)}, u32[]{:S(2)}) collective-permute-start(s32[32,8]{0,1:T(8,128)S(1)} %collective-permute-done.6), channel_id=1, source_target_pairs={{0,2},{2,4},{4,6},{6,8},{8,10},{10,12},{12,14},{14,16},{16,18},{18... | collective-permute-start | bytes 3080 | tf_op jit(solution)/shard_map/ppermute | solution.py:14
  103.0 7.2 %collective-permute-start.8 = (s32[32,8]{0,1:T(8,128)S(1)}, s32[32,8]{0,1:T(8,128)S(1)}, u32[]{:S(2)}, u32[]{:S(2)}) collective-permute-start(s32[32,8]{0,1:T(8,128)S(1)} %collective-permute-done.7), channel_id=1, source_target_pairs={{0,2},{2,4},{4,6},{6,8},{8,10},{10,12},{12,14},{14,16},{16,18},{18... | collective-permute-start | bytes 3080 | tf_op jit(solution)/shard_map/ppermute | solution.py:14
  110.2 7.3 %collective-permute-start.9 = (s32[32,8]{0,1:T(8,128)S(1)}, s32[32,8]{0,1:T(8,128)S(1)}, u32[]{:S(2)}, u32[]{:S(2)}) collective-permute-start(s32[32,8]{0,1:T(8,128)S(1)} %collective-permute-done.8), channel_id=1, source_target_pairs={{0,2},{2,4},{4,6},{6,8},{8,10},{10,12},{12,14},{14,16},{16,18},{18... | collective-permute-start | bytes 3080 | tf_op jit(solution)/shard_map/ppermute | solution.py:14
  117.5 7.2 %collective-permute-start.10 = (s32[32,8]{0,1:T(8,128)S(1)}, s32[32,8]{0,1:T(8,128)S(1)}, u32[]{:S(2)}, u32[]{:S(2)}) collective-permute-start(s32[32,8]{0,1:T(8,128)S(1)} %collective-permute-done.9), channel_id=1, source_target_pairs={{0,2},{2,4},{4,6},{6,8},{8,10},{10,12},{12,14},{14,16},{16,18},{18... | collective-permute-start | bytes 3080 | tf_op jit(solution)/shard_map/ppermute | solution.py:14
  124.7 7.2 %collective-permute-start.11 = (s32[32,8]{0,1:T(8,128)S(1)}, s32[32,8]{0,1:T(8,128)S(1)}, u32[]{:S(2)}, u32[]{:S(2)}) collective-permute-start(s32[32,8]{0,1:T(8,128)S(1)} %collective-permute-done.10), channel_id=1, source_target_pairs={{0,2},{2,4},{4,6},{6,8},{8,10},{10,12},{12,14},{14,16},{16,18},{18... | collective-permute-start | bytes 3080 | tf_op jit(solution)/shard_map/ppermute | solution.py:14
  131.9 7.4 %collective-permute-start.12 = (s32[32,8]{0,1:T(8,128)S(1)}, s32[32,8]{0,1:T(8,128)S(1)}, u32[]{:S(2)}, u32[]{:S(2)}) collective-permute-start(s32[32,8]{0,1:T(8,128)S(1)} %collective-permute-done.11), channel_id=1, source_target_pairs={{0,2},{2,4},{4,6},{6,8},{8,10},{10,12},{12,14},{14,16},{16,18},{18... | collective-permute-start | bytes 3080 | tf_op jit(solution)/shard_map/ppermute | solution.py:14
  139.3 7.4 %collective-permute-start.13 = (s32[32,8]{0,1:T(8,128)S(1)}, s32[32,8]{0,1:T(8,128)S(1)}, u32[]{:S(2)}, u32[]{:S(2)}) collective-permute-start(s32[32,8]{0,1:T(8,128)S(1)} %collective-permute-done.12), channel_id=1, source_target_pairs={{0,2},{2,4},{4,6},{6,8},{8,10},{10,12},{12,14},{14,16},{16,18},{18... | collective-permute-start | bytes 3080 | tf_op jit(solution)/shard_map/ppermute | solution.py:14
  146.8 7.3 %collective-permute-start.14 = (s32[32,8]{0,1:T(8,128)S(1)}, s32[32,8]{0,1:T(8,128)S(1)}, u32[]{:S(2)}, u32[]{:S(2)}) collective-permute-start(s32[32,8]{0,1:T(8,128)S(1)} %collective-permute-done.13), channel_id=1, source_target_pairs={{0,2},{2,4},{4,6},{6,8},{8,10},{10,12},{12,14},{14,16},{16,18},{18... | collective-permute-start | bytes 3080 | tf_op jit(solution)/shard_map/ppermute | solution.py:14
  154.3 9.4 %copy-start = (bf16[512,3584]{1,0:T(8,128)(2,1)S(1)}, bf16[512,3584]{1,0:T(8,128)(2,1)}, u32[]{:S(2)}) copy-start(bf16[512,3584]{1,0:T(8,128)(2,1)} %all-gather.4.cloned.1.call-done) | copy-start | bytes 11010052
  180.3 119.4 %reduce-scatter.3.cloned.1.call-start = ((), (), s32[]{:S(2)}) async-start(), calls=%async_computation.3 | async-start | bytes 3899392 | tf_op jit(solution)/shard_map/reduce_scatter | solution.py:50
  212.7 11.7 %slice-start = ((s8[7340032]{0:T(1024)(128)(4,1)}), s8[3145728]{0:T(1024)(128)(4,1)S(1)}, s32[]{:S(2)}) async-start(s8[7340032]{0:T(1024)(128)(4,1)} %bitcast.32), calls=%async_computation.7 | async-start | bytes 6291456
  212.7 174.3 %reduce-scatter.5.cloned.1.call-start = ((), (), s32[]{:S(2)}) async-start(), calls=%async_computation.5 | async-start | bytes 3899392 | tf_op jit(solution)/shard_map/reduce_scatter | solution.py:51
  212.8 11.6 %slice-start.1 = ((s8[7340032]{0:T(1024)(128)(4,1)}), s8[4194304]{0:T(1024)(128)(4,1)S(1)}, s32[]{:S(2)}) async-start(s8[7340032]{0:T(1024)(128)(4,1)} %bitcast.32), calls=%async_computation.8 | async-start | bytes 8388608
  212.8 11.6 %copy-start.1 = (bf16[512,1024]{1,0:T(8,128)(2,1)S(1)}, bf16[512,1024]{1,0:T(8,128)(2,1)}, u32[]{:S(2)}) copy-start(bf16[512,1024]{1,0:T(8,128)(2,1)} %get-tuple-element.3) | copy-start | bytes 3145732
  212.8 11.6 %copy-start.2 = (bf16[512,1024]{1,0:T(8,128)(2,1)S(1)}, bf16[512,1024]{1,0:T(8,128)(2,1)}, u32[]{:S(2)}) copy-start(bf16[512,1024]{1,0:T(8,128)(2,1)} %get-tuple-element.4) | copy-start | bytes 3145732
Sparse Core Ops, SparseCore 0:
  10.7 74.8 all-gather.3
  88.4 70.3 all-gather.5
  180.4 22.3 all-reduce.2
  212.8 86.8 reduce-scatter.2
  302.5 84.5 reduce-scatter.4
